TPU v7x, 512 devices: a whole 4x4x16 slice. The times are simulated.
512 devices in a mesh: seq: 64 (over z, y_lo, core), head: 8 (over x, y_hi).
Axes of the slice: x: 4, y: 4 (y_hi: 2, y_lo: 2; y = y_hi * 2 + y_lo), z: 16, core: 2. Of those that a mesh axis runs over, the one named last changes fastest.
Arguments:
- queries: bfloat16 [4096, 3072], P('seq', 'head'), may hold values from -10 to 10
- suffix_latent: bfloat16 [4096, 576], P('seq'), may hold values from -6 to 6
- prefix_latent: bfloat16 [1024, 576], P('seq'), may hold values from -6 to 6
- kv_up: bfloat16 [16, 512, 256], P('head'), may hold values from -0.25 to 0.25
- w_out: bfloat16 [2048, 2048], P('head'), may hold values from -2 to 2
- residual: bfloat16 [4096, 2048], P('seq'), may hold values from -400 to 400
- norm_gain: bfloat16 [2048], replicated, may hold values from 0.099609375 to 1.8984375
- router: bfloat16 [2048, 64], replicated, may hold values from -0.125 to 0.125
- w_gate: bfloat16 [64, 2048, 1408], P('seq', None, 'head'), may hold values from -0.125 to 0.125
- w_up: bfloat16 [64, 2048, 1408], P('seq', None, 'head'), may hold values from -0.125 to 0.125
- w_down: bfloat16 [64, 1408, 2048], P('seq', 'head'), may hold values from -0.15625 to 0.15625
- lengths: int32 [128], replicated, may hold values from 1 to 64, 4096 in all
- group_map: int32 [128], replicated, may hold values from 0 to 1
- expert_ids: int32 [4096, 6], P('seq'), may hold values from 0 to 63, all different within a row; in each aligned block of 64 rows (0 to 63, 64 to 127, ...) at most 9 rows name the same one
Outputs:
- attention: bfloat16 [4096, 2048], P('seq', 'head')
- expert_out: bfloat16 [4096, 2048], P('seq', 'head')
Inputs may be any that keep to these rules, and one draw needn't show every extreme that they name: `lengths`: the requests cover the 4096 tokens exactly; each has 1 to 64 tokens, and one has exactly 64. `expert_ids`: each token names 6 different experts. Among the 64 tokens of one index of seq (aligned blocks of rows) no expert is named more than 9 times, a bound that some block reaches.
All inputs are finite; a program needn't handle non-finite values.
Results may differ from a plain program's by a relative error of at most 0.027.
Values may be sent and summed in bfloat16 or wider, within the bound.
A program may use at most 64 MiB of HBM per device.

v0:
```python
import math
import jax
import jax.numpy as jnp
from jax import lax
from jax.sharding import PartitionSpec as P

D = 2048
NOPE = 128
ROPE = 64
VDIM = 128
LAT = 512
TOPK = 6
PRE_LEN = 512
score_scale = 1.0 / math.sqrt(192.0)
route_scale = 2.446
norm_eps = 1e-06


def shifted(value, axis, by):
    peers = lax.axis_size(axis)
    pairs = [(i, i + by) for i in range(peers) if 0 <= i + by < peers]
    return lax.ppermute(value, axis, pairs)


def request_info(lengths, group_map, position):
    request_ends = jnp.cumsum(lengths)
    request_starts = request_ends - lengths
    request_index = jnp.sum((request_ends[None, :] <= position[:, None]).astype(jnp.int32), axis=1)
    member = (
        request_index[:, None] == jnp.arange(lengths.shape[0], dtype=jnp.int32)[None, :]
    ).astype(jnp.int32)
    first_token = jnp.sum(member * request_starts[None, :], axis=1)
    token_group = jnp.sum(member * group_map[None, :], axis=1)
    return (first_token, token_group)


def on_device(
    queries,
    suffix_latent,
    prefix_latent,
    kv_up,
    w_out,
    residual,
    norm_gain,
    router,
    w_gate,
    w_up,
    w_down,
    lengths,
    group_map,
    expert_ids,
):
    tok_count = queries.shape[0]
    head_local = kv_up.shape[0]
    seq_index = lax.axis_index("seq")
    first_row = seq_index * tok_count
    position = first_row + jnp.arange(tok_count, dtype=jnp.int32)
    first_token, token_group = request_info(lengths, group_map, position)
    query_block = queries.reshape(tok_count, head_local, NOPE + ROPE)
    absorbed = jnp.einsum(
        "thn,hln->thl",
        query_block[:, :, :NOPE],
        kv_up[:, :, :NOPE],
        preferred_element_type=jnp.float32,
    ).astype(jnp.bfloat16)
    joined = jnp.concatenate([absorbed, query_block[:, :, NOPE:]], axis=2).reshape(
        tok_count * head_local, LAT + ROPE
    )
    earlier = shifted(suffix_latent, "seq", 1)
    nearby = jnp.concatenate([earlier, suffix_latent], axis=0)
    near_pos = first_row - tok_count + jnp.arange(2 * tok_count, dtype=jnp.int32)
    near_seen = (near_pos[None, :] >= first_token[:, None]) & (
        near_pos[None, :] <= position[:, None]
    )
    near_seen = jnp.repeat(near_seen, head_local, axis=0)
    scores = jnp.dot(joined, nearby.T, preferred_element_type=jnp.float32) * score_scale
    row_max = jnp.max(jnp.where(near_seen, scores, -jnp.inf), axis=1, keepdims=True)
    weights = jnp.where(near_seen, jnp.exp(scores - row_max), 0.0)
    total = jnp.sum(weights, axis=1, keepdims=True)
    weighted = jnp.dot(
        weights.astype(jnp.bfloat16), nearby[:, :LAT], preferred_element_type=jnp.float32
    )
    group_rows = jnp.repeat(token_group, head_local)
    piece = lax.all_gather(prefix_latent, "seq", axis=0, tiled=True)
    row_group = jnp.arange(piece.shape[0], dtype=jnp.int32) // PRE_LEN
    visible = row_group[None, :] == group_rows[:, None]
    piece_scores = jnp.dot(joined, piece.T, preferred_element_type=jnp.float32) * score_scale
    new_max = jnp.maximum(
        row_max, jnp.max(jnp.where(visible, piece_scores, -jnp.inf), axis=1, keepdims=True)
    )
    piece_weights = jnp.where(visible, jnp.exp(piece_scores - new_max), 0.0)
    factor = jnp.exp(row_max - new_max)
    new_total = total * factor + jnp.sum(piece_weights, axis=1, keepdims=True)
    new_weighted = weighted * factor + jnp.dot(
        piece_weights.astype(jnp.bfloat16), piece[:, :LAT], preferred_element_type=jnp.float32
    )
    mixed = (new_weighted / new_total).astype(jnp.bfloat16).reshape(tok_count, head_local, LAT)
    heads_out = jnp.einsum(
        "thl,hlv->thv", mixed, kv_up[:, :, NOPE:], preferred_element_type=jnp.float32
    ).astype(jnp.bfloat16)
    partial_value = jnp.dot(
        heads_out.reshape(tok_count, head_local * VDIM), w_out, preferred_element_type=jnp.float32
    )
    col_width = D // lax.axis_size("head")
    col_start = lax.axis_index("head") * col_width
    attention_sum = lax.psum(partial_value.astype(jnp.bfloat16), "head").astype(jnp.float32)
    attention = lax.dynamic_slice_in_dim(attention_sum, col_start, col_width, 1).astype(
        jnp.bfloat16
    )
    hidden_state = residual.astype(jnp.float32) + attention_sum
    mean_square = jnp.mean(hidden_state * hidden_state, axis=1, keepdims=True)
    normed = (
        hidden_state * lax.rsqrt(mean_square + norm_eps) * norm_gain.astype(jnp.float32)
    ).astype(jnp.bfloat16)
    logits = jnp.dot(normed, router, preferred_element_type=jnp.float32)
    expert_count = router.shape[1]
    capacity = (3 * tok_count * TOPK + 2 * expert_count - 1) // (2 * expert_count)
    member = expert_ids[:, :, None] == jnp.arange(expert_count, dtype=jnp.int32)[None, None, :]
    chosen = jnp.sum(jnp.where(member, jax.nn.sigmoid(logits)[:, None, :], 0.0), axis=2)
    gates = chosen / jnp.sum(chosen, axis=1, keepdims=True) * route_scale
    flat_member = member.reshape(tok_count * TOPK, expert_count).astype(jnp.int32)
    running = jnp.cumsum(flat_member, axis=0)
    slot_rank = jnp.sum(flat_member * running, axis=1) - 1
    slot_index = expert_ids.reshape(-1) * capacity + slot_rank
    pair_token = jnp.arange(tok_count * TOPK, dtype=jnp.int32) // TOPK
    source_row = jnp.zeros((expert_count * capacity,), jnp.int32).at[slot_index].set(pair_token + 1)
    padded_rows = jnp.concatenate([jnp.zeros((1, normed.shape[1]), jnp.bfloat16), normed], axis=0)
    outgoing = padded_rows[source_row].reshape(expert_count, capacity, normed.shape[1])
    local_experts = w_gate.shape[0]
    received = lax.all_to_all(outgoing, "seq", split_axis=0, concat_axis=0, tiled=True)
    shaped = received.reshape(-1, local_experts, received.shape[1], received.shape[2])
    gate_part = jnp.einsum("secd,edf->secf", shaped, w_gate, preferred_element_type=jnp.float32)
    up_part = jnp.einsum("secd,edf->secf", shaped, w_up, preferred_element_type=jnp.float32)
    inner = (jax.nn.silu(gate_part) * up_part).astype(jnp.bfloat16)
    down_part = jnp.einsum(
        "secf,efd->secd", inner, w_down, preferred_element_type=jnp.float32
    ).astype(jnp.bfloat16)
    produced = down_part.reshape(-1, down_part.shape[2], down_part.shape[3])
    returned = lax.all_to_all(produced, "seq", split_axis=0, concat_axis=0, tiled=True)
    picked = returned.reshape(expert_count * capacity, returned.shape[2])[slot_index].reshape(
        tok_count, TOPK, returned.shape[2]
    )
    combined = jnp.sum(picked.astype(jnp.float32) * gates[:, :, None], axis=1)
    expert_out = lax.psum_scatter(
        combined.astype(jnp.bfloat16), "head", scatter_dimension=1, tiled=True
    )
    return (attention, expert_out)


def solution(mesh):
    placed = (
        P("seq", "head"),
        P("seq", None),
        P("seq", None),
        P("head", None, None),
        P("head", None),
        P("seq", None),
        P(),
        P(),
        P("seq", None, "head"),
        P("seq", None, "head"),
        P("seq", "head", None),
        P(),
        P(),
        P("seq", None),
    )
    return jax.shard_map(
        on_device,
        mesh=mesh,
        in_specs=placed,
        out_specs=(P("seq", "head"), P("seq", "head")),
        check_vma=False,
    )
```

profile of v0, /device:TPU:2, one launch (start us, length us, event | category | flops | bytes accessed | tf_op | source)
XLA Modules:
  0.0 760.6 jit_solution(14834072606422764430)
XLA Ops:
  7.2 0.7 all-gather.2.cloned.1.call-update
  8.0 1.7 collective-permute-start
  9.7 0.7 broadcast_multiply_fusion
  10.4 0.8 copy.50
  11.2 0.2 reduce-window.18
  11.5 0.2 convert_reduce_fusion
  11.7 0.8 copy.59
  12.6 0.1 eq.67
  12.7 0.9 reshape.210
  13.7 0.7 sub.51
  14.4 0.7 convert_element_type.78
  15.1 0.1 mul.133
  15.3 0.8 select_reduce_fusion.3
  16.5 0.1 eq.64
  16.7 0.9 reduce-window.19
  17.6 0.2 slice_reduce_fusion
  17.9 1.2 fusion.10
  19.0 0.2 copy.53
  19.5 2.9 scatter_custom_fusion
  22.5 0.2 select_reduce_fusion.2
  22.8 113.3 %all-gather.2.cloned.1.call-done = bf16[1024,576]{1,0:T(8,128)(2,1)} async-done(((bf16[16,576]{1,0:T(8,128)(2,1)}), bf16[1024,576]{1,0:T(8,128)(2,1)}) %all-gather.2.cloned.1.call-update) | async-done | bytes 1179664 | tf_op jit(solution)/shard_map/all_gather | solution.py:84
  136.1 2.1 fusion.26
  138.2 0.3 fusion.27
  138.5 0.4 fusion.15
  138.8 0.2 fusion.7
  139.2 0.2 fusion.11
  139.4 1.0 convolution_convert_fusion.1
  140.4 95.5 %all-reduce.3.cloned.1.call-done = bf16[64,2048]{1,0:T(8,128)(2,1)} async-done(((bf16[64,2048]{1,0:T(8,128)(2,1)}), bf16[64,2048]{1,0:T(8,128)(2,1)}) %all-reduce.3.cloned.1.call-update) | async-done | bytes 262160 | tf_op jit(solution)/shard_map/psum | solution.py:106
  235.9 1.1 multiply_reduce_fusion.1
  237.1 1.1 multiply_convert_fusion
  238.1 0.7 copy-done.4
  238.9 4.0 gather_fusion
  242.9 4.6 reshape.215
  247.5 204.3 %all_to_all.10 = bf16[64,9,2048]{2,1,0:T(8,128)(2,1)S(1)} all-to-all(bf16[64,9,2048]{2,1,0:T(8,128)(2,1)} %reshape.215), channel_id=1, replica_groups=mesh['seq'=64,'head'=8] {'seq'}, dimensions={0} | all-to-all | bytes 4718592 | tf_op jit(solution)/shard_map/all_to_all | solution.py:130
  451.8 1.9 copy-done.1
  453.7 3.5 convolution_bitcast_fusion.1
  457.2 5.6 convolution_convert_fusion
  462.8 3.5 copy.64
  466.3 5.8 all-to-all-start.1
  472.2 0.2 fusion.14
  472.4 0.3 select_reduce_fusion
  472.8 190.1 %all-to-all-done.1 = bf16[64,9,2048]{2,1,0:T(8,128)(2,1)} async-done(((bf16[64,9,2048]{2,1,0:T(8,128)(2,1)}), bf16[64,9,2048]{2,1,0:T(8,128)(2,1)}, u32[]{:S(2)}, u32[]{:S(2)}) %all-to-all-start.1) | async-done | bytes 2359328 | tf_op jit(solution)/shard_map/all_to_all | solution.py:139
  662.9 3.4 reshape.220
  666.3 3.1 gather_fusion.1
  669.4 3.9 reshape.221
  673.3 4.5 multiply_reduce_fusion
  677.8 1.4 dynamic-slice_convert_fusion
  679.1 74.9 %reduce-scatter.2.cloned.1.call-done = bf16[64,256]{1,0:T(8,128)(2,1)} async-done(((bf16[64,2048]{1,0:T(8,128)(2,1)}), bf16[64,256]{1,0:T(8,128)(2,1)}) %reduce-scatter.2.cloned.1.call-update) | async-done | bytes 32784 | tf_op jit(solution)/shard_map/reduce_scatter | solution.py:144
  (61 shorter events, 1.7 us)
Async XLA Ops:
  7.2 132.2 %copy-start = (bf16[256,2048]{1,0:T(8,128)(2,1)S(1)}, bf16[256,2048]{1,0:T(8,128)(2,1)}, u32[]{:S(2)}) copy-start(bf16[256,2048]{1,0:T(8,128)(2,1)} %param.18) | copy-start | bytes 3145732
  7.2 15.3 %copy-start.7 = (bf16[64,576]{1,0:T(8,128)(2,1)S(1)}, bf16[64,576]{1,0:T(8,128)(2,1)}, u32[]{:S(2)}) copy-start(bf16[64,576]{1,0:T(8,128)(2,1)} %param.15) | copy-start | bytes 221188
  7.2 128.9 %all-gather.2.cloned.1.call-start = ((), (), s32[]{:S(2)}) async-start(), calls=%async_computation.3 | async-start | bytes 1331200 | tf_op jit(solution)/shard_map/all_gather | solution.py:84
  7.9 228.0 %all-reduce.3.cloned.1.call-start = ((), (), s32[]{:S(2)}) async-start(), calls=%async_computation.4 | async-start | bytes 524288 | tf_op jit(solution)/shard_map/psum | solution.py:106
  8.0 14.5 %collective-permute-start = (bf16[64,576]{1,0:T(8,128)(2,1)}, bf16[64,576]{1,0:T(8,128)(2,1)S(1)}, u32[]{:S(2)}, u32[]{:S(2)}) collective-permute-start(bf16[64,576]{1,0:T(8,128)(2,1)} %param.15), channel_id=1, source_target_pairs={{0,8},{8,16},{16,24},{24,32},{32,40},{40,48},{48,56},{56,64},{64,7... | collective-permute-start | bytes 221192 | tf_op jit(solution)/shard_map/ppermute | solution.py:22
  136.1 2.4 copy-start.2
  138.2 1.0 copy-start.6
  138.5 97.5 %copy-start.3 = (bf16[64,2048]{1,0:T(8,128)(2,1)S(1)}, bf16[64,2048]{1,0:T(8,128)(2,1)}, u32[]{:S(2)}) copy-start(bf16[64,2048]{1,0:T(8,128)(2,1)} %param.19) | copy-start | bytes 786436
  238.1 0.7 copy-start.4
  247.5 206.2 %copy-start.9 = (bf16[1,2048,176]{1,2,0:T(8,128)(2,1)S(1)}, bf16[1,2048,176]{1,2,0:T(8,128)(2,1)}, u32[]{:S(2)}) copy-start(bf16[1,2048,176]{1,2,0:T(8,128)(2,1)} %param.22) | copy-start | bytes 2162692
  451.8 1.9 copy-start.1
  466.3 5.9 copy-start.5
  466.3 5.9 copy-start.10
  466.3 6.1 copy-start.8
  466.3 196.6 %all-to-all-start.1 = ((bf16[64,9,2048]{2,1,0:T(8,128)(2,1)}), bf16[64,9,2048]{2,1,0:T(8,128)(2,1)}, u32[]{:S(2)}, u32[]{:S(2)}) async-start(bf16[64,9,2048]{2,1,0:T(8,128)(2,1)} %copy.64), calls=%async_computation.1 | async-start | bytes 8388608 | tf_op jit(solution)/shard_map/all_to_all | solution.py:139
  472.1 282.0 %reduce-scatter.2.cloned.1.call-start = ((), (), s32[]{:S(2)}) async-start(), calls=%async_computation.5 | async-start | bytes 294912 | tf_op jit(solution)/shard_map/reduce_scatter | solution.py:144
Sparse Core Ops, SparseCore 0:
  10.1 125.8 all-gather.1
  140.5 95.3 all-reduce.2
  677.9 76.1 reduce-scatter.1
where the time goes:
time: 762 us; the launch traced here: 761 us
  waiting for transfers between devices  475 us (62%)
  blocking collectives  204 us (27%)
  local copies, waits for them, and re-layouts  33.7 us (4%)
  matrix products  14.5 us (2%)
  between operations  14.2 us (2%)
  other arithmetic  11.8 us (2%)
  starting transfers between devices  7.65 us (1%)
    all_to_all x1, blocking collectives, on_device(): lax.all_to_all(outgoing, 'seq', split_axis=0, concat_axis=0, tiled=True)  204 us
    all_to_all x1, waiting for transfers between devices, on_device(): lax.all_to_all(produced, 'seq', split_axis=0, concat_axis=0, tiled=True)  190 us
    all_gather x1, waiting for transfers between devices, on_device(): piece = lax.all_gather(prefix_latent, 'seq', axis=0, tiled=True)  113 us
    psum x1, waiting for transfers between devices, on_device(): lax.psum(partial_value.astype(jnp.bfloat16), 'head').astype(jnp.float32)  95.5 us
    reduce_scatter x1, waiting for transfers between devices, on_device(): lax.psum_scatter(combined.astype(jnp.bfloat16), 'head', scatter_dimension...  74.9 us
  transfers between devices with their start and end apart: 5, of which 4 were waited for; matrix products, arithmetic and copies ran while one was open for 2% of the time, Pallas kernels for 0%

commit v1 on v0

--- a/solution.py
+++ b/solution.py
@@ -14,6 +14,17 @@
 score_scale = 1.0 / math.sqrt(192.0)
 route_scale = 2.446
 norm_eps = 1e-06
+
+
+def hold_series_all(field_in, along_axis):
+    parts_seen = []
+    for _ in range(lax.axis_size(along_axis)):
+        parts_seen.append(field_in)
+    finding = jnp.concatenate(
+        lax.all_to_all(jnp.stack(parts_seen), axis_name=along_axis, split_axis=0, concat_axis=0),
+        axis=0,
+    )
+    return finding
 
 
 def shifted(value, axis, by):
@@ -81,7 +92,7 @@
         weights.astype(jnp.bfloat16), nearby[:, :LAT], preferred_element_type=jnp.float32
     )
     group_rows = jnp.repeat(token_group, head_local)
-    piece = lax.all_gather(prefix_latent, "seq", axis=0, tiled=True)
+    piece = hold_series_all(prefix_latent, along_axis="seq")
     row_group = jnp.arange(piece.shape[0], dtype=jnp.int32) // PRE_LEN
     visible = row_group[None, :] == group_rows[:, None]
     piece_scores = jnp.dot(joined, piece.T, preferred_element_type=jnp.float32) * score_scale

time: 762 us -> 714 us (0.937)
  waiting for transfers between devices: 475 us -> 415 us
  starting transfers between devices: 7.65 us -> 24.9 us
    all_gather x1 -> x0, waiting for transfers between devices: 113 us -> none  [on_device(): piece = lax.all_gather(prefix_latent, 'seq', axis=0, tiled=True)]
    all_to_all x0 -> x1, waiting for transfers between devices: none -> 58 us  [hold_series_all(): lax.all_to_all(jnp.stack(parts_seen), axis_name=along_axis, split_axis=0,...]
    all_to_all x0 -> x1, starting transfers between devices: none -> 17.1 us  [hold_series_all(): lax.all_to_all(jnp.stack(parts_seen), axis_name=along_axis, split_axis=0,...]
  transfers between devices with their start and end apart: 5 -> 5, of which waited for: 4 -> 4; matrix products, arithmetic and copies ran while one was open for 2% -> 1% of each run, Pallas kernels for 0% -> 0%
where the time goes in v1:
time: 714 us
  waiting for transfers between devices  415 us (58%)
  blocking collectives  204 us (29%)
  local copies, waits for them, and re-layouts  33.5 us (5%)
  starting transfers between devices  24.9 us (3%)
  between operations  14.6 us (2%)
  matrix products  12.1 us (2%)
  other arithmetic  9.12 us (1%)
    all_to_all x1, blocking collectives, on_device(): lax.all_to_all(outgoing, 'seq', split_axis=0, concat_axis=0, tiled=True)  204 us
    all_to_all x1, waiting for transfers between devices, on_device(): lax.all_to_all(produced, 'seq', split_axis=0, concat_axis=0, tiled=True)  190 us
    psum x1, waiting for transfers between devices, on_device(): lax.psum(partial_value.astype(jnp.bfloat16), 'head').astype(jnp.float32)  92 us
    reduce_scatter x1, waiting for transfers between devices, on_device(): lax.psum_scatter(combined.astype(jnp.bfloat16), 'head', scatter_dimension...  75 us
    all_to_all x1, waiting for transfers between devices, hold_series_all(): lax.all_to_all(jnp.stack(parts_seen), axis_name=along_axis, split_axis=0,...  58 us
    all_to_all x1, starting transfers between devices, hold_series_all(): lax.all_to_all(jnp.stack(parts_seen), axis_name=along_axis, split_axis=0,...  17.1 us
  transfers between devices with their start and end apart: 5, of which 4 were waited for; matrix products, arithmetic and copies ran while one was open for 1% of the time, Pallas kernels for 0%

profile of v1, /device:TPU:2, one launch (start us, length us, event | category | flops | bytes accessed | tf_op | source)
XLA Modules:
  0.0 713.6 jit_solution(13920339339650264264)
XLA Ops:
  7.3 2.0 stack.2
  9.3 17.1 %all-to-all-start = ((bf16[64,16,576]{2,1,0:T(8,128)(2,1)}), bf16[64,16,576]{2,1,0:T(8,128)(2,1)S(1)}, u32[]{:S(2)}, u32[]{:S(2)}) async-start(bf16[64,16,576]{2,1,0:T(8,128)(2,1)} %stack.2), calls=%async_computation | async-start | bytes 2621440 | tf_op jit(solution)/shard_map/all_to_all | solution.py:24
  26.4 2.0 collective-permute-start
  28.5 0.1 eq.71
  28.7 0.1 eq.67
  29.1 0.1 mul.133
  29.3 0.1 copy.50
  29.4 0.2 reduce-window.18
  29.6 0.1 reduce.1
  29.7 0.2 convert_reduce_fusion
  29.9 0.2 select_reduce_fusion.3
  30.3 0.1 copy.55
  30.4 0.1 eq.64
  30.6 0.9 reduce-window.19
  31.5 0.2 slice_reduce_fusion
  31.8 0.2 fusion.10
  32.0 0.2 copy.53
  32.2 0.1 reshape.216
  32.5 2.9 scatter_custom_fusion
  35.5 0.2 select_reduce_fusion.2
  35.8 58.0 %all-to-all-done = bf16[64,16,576]{2,1,0:T(8,128)(2,1)S(1)} async-done(((bf16[64,16,576]{2,1,0:T(8,128)(2,1)}), bf16[64,16,576]{2,1,0:T(8,128)(2,1)S(1)}, u32[]{:S(2)}, u32[]{:S(2)}) %all-to-all-start) | async-done | bytes 1179680 | tf_op jit(solution)/shard_map/all_to_all | solution.py:24
  93.7 0.6 fusion.26
  94.4 0.4 fusion.15
  94.8 0.3 fusion.27
  95.1 0.2 fusion.7
  95.4 0.2 fusion.11
  95.5 1.0 convolution_convert_fusion.1
  96.6 92.0 %all-reduce.3.cloned.1.call-done = bf16[64,2048]{1,0:T(8,128)(2,1)} async-done(((bf16[64,2048]{1,0:T(8,128)(2,1)}), bf16[64,2048]{1,0:T(8,128)(2,1)}) %all-reduce.3.cloned.1.call-update) | async-done | bytes 262160 | tf_op jit(solution)/shard_map/psum | solution.py:117
  188.5 1.1 multiply_reduce_fusion.1
  189.7 1.1 multiply_convert_fusion
  190.8 0.7 copy-done.3
  191.6 4.0 gather_fusion
  195.5 4.6 reshape.221
  200.1 204.3 %all_to_all.15 = bf16[64,9,2048]{2,1,0:T(8,128)(2,1)S(1)} all-to-all(bf16[64,9,2048]{2,1,0:T(8,128)(2,1)} %reshape.221), channel_id=1, replica_groups=mesh['seq'=64,'head'=8] {'seq'}, dimensions={0} | all-to-all | bytes 4718592 | tf_op jit(solution)/shard_map/all_to_all | solution.py:141
  404.5 1.9 copy-done.1
  406.4 3.5 convolution_bitcast_fusion.1
  409.9 5.6 convolution_convert_fusion
  415.4 3.5 copy.64
  418.9 5.8 all-to-all-start.2
  424.8 0.2 fusion.14
  425.0 0.3 select_reduce_fusion
  425.4 190.1 %all-to-all-done.2 = bf16[64,9,2048]{2,1,0:T(8,128)(2,1)} async-done(((bf16[64,9,2048]{2,1,0:T(8,128)(2,1)}), bf16[64,9,2048]{2,1,0:T(8,128)(2,1)}, u32[]{:S(2)}, u32[]{:S(2)}) %all-to-all-start.2) | async-done | bytes 2359328 | tf_op jit(solution)/shard_map/all_to_all | solution.py:150
  615.5 3.4 reshape.226
  618.9 3.1 gather_fusion.1
  622.0 3.9 reshape.227
  625.9 4.5 multiply_reduce_fusion
  630.4 1.4 dynamic-slice_convert_fusion
  631.8 75.0 %reduce-scatter.2.cloned.1.call-done = bf16[64,256]{1,0:T(8,128)(2,1)} async-done(((bf16[64,2048]{1,0:T(8,128)(2,1)}), bf16[64,256]{1,0:T(8,128)(2,1)}) %reduce-scatter.2.cloned.1.call-update) | async-done | bytes 32784 | tf_op jit(solution)/shard_map/reduce_scatter | solution.py:155
  (67 shorter events, 1.3 us)
Async XLA Ops:
  7.2 88.4 %copy-start = (bf16[256,2048]{1,0:T(8,128)(2,1)S(1)}, bf16[256,2048]{1,0:T(8,128)(2,1)}, u32[]{:S(2)}) copy-start(bf16[256,2048]{1,0:T(8,128)(2,1)} %param.18) | copy-start | bytes 3145732
  7.2 19.2 %copy-start.6 = (bf16[64,576]{1,0:T(8,128)(2,1)S(1)}, bf16[64,576]{1,0:T(8,128)(2,1)}, u32[]{:S(2)}) copy-start(bf16[64,576]{1,0:T(8,128)(2,1)} %param.15) | copy-start | bytes 221188
  7.2 21.2 %copy-start.8 = (s32[64,6]{0,1:T(8,128)S(1)}, s32[64,6]{0,1:T(8,128)}, u32[]{:S(2)}) copy-start(s32[64,6]{0,1:T(8,128)} %param.27) | copy-start | bytes 4612
  7.2 21.6 %copy-start.7 = (bf16[64,384]{1,0:T(8,128)(2,1)S(1)}, bf16[64,384]{1,0:T(8,128)(2,1)}, u32[]{:S(2)}) copy-start(bf16[64,384]{1,0:T(8,128)(2,1)} %param.14) | copy-start | bytes 147460
  7.2 21.8 %copy-start.9 = (bf16[2048]{0:T(1024)(128)(2,1)S(1)}, bf16[2048]{0:T(1024)(128)(2,1)}, u32[]{:S(2)}) copy-start(bf16[2048]{0:T(1024)(128)(2,1)} %param.20) | copy-start | bytes 12292
  7.2 22.0 %copy-start.10 = (s32[128]{0:T(128)S(1)}, s32[128]{0:T(128)}, u32[]{:S(2)}) copy-start(s32[128]{0:T(128)} %param.25) | copy-start | bytes 1540
  7.2 22.7 %copy-start.11 = (s32[128]{0:T(128)S(1)}, s32[128]{0:T(128)}, u32[]{:S(2)}) copy-start(s32[128]{0:T(128)} %param.26) | copy-start | bytes 1540
  7.2 24.5 %copy-start.5 = (bf16[2,512,256]{2,1,0:T(8,128)(2,1)S(1)}, bf16[2,512,256]{2,1,0:T(8,128)(2,1)}, u32[]{:S(2)}) copy-start(bf16[2,512,256]{2,1,0:T(8,128)(2,1)} %param.17) | copy-start | bytes 1572868
  9.3 84.5 %all-to-all-start = ((bf16[64,16,576]{2,1,0:T(8,128)(2,1)}), bf16[64,16,576]{2,1,0:T(8,128)(2,1)S(1)}, u32[]{:S(2)}, u32[]{:S(2)}) async-start(bf16[64,16,576]{2,1,0:T(8,128)(2,1)} %stack.2), calls=%async_computation | async-start | bytes 2621440 | tf_op jit(solution)/shard_map/all_to_all | solution.py:24
  26.4 162.2 %all-reduce.3.cloned.1.call-start = ((), (), s32[]{:S(2)}) async-start(), calls=%async_computation.4 | async-start | bytes 524288 | tf_op jit(solution)/shard_map/psum | solution.py:117
  26.4 9.0 %collective-permute-start = (bf16[64,576]{1,0:T(8,128)(2,1)S(1)}, bf16[64,576]{1,0:T(8,128)(2,1)S(1)}, u32[]{:S(2)}, u32[]{:S(2)}) collective-permute-start(bf16[64,576]{1,0:T(8,128)(2,1)S(1)} %copy-done.6), channel_id=1, source_target_pairs={{0,8},{8,16},{16,24},{24,32},{32,40},{40,48},{48,56},{56,64},{64,7... | collective-permute-start | bytes 221192 | tf_op jit(solution)/shard_map/ppermute | solution.py:33
  94.8 93.8 %copy-start.2 = (bf16[64,2048]{1,0:T(8,128)(2,1)S(1)}, bf16[64,2048]{1,0:T(8,128)(2,1)}, u32[]{:S(2)}) copy-start(bf16[64,2048]{1,0:T(8,128)(2,1)} %param.19) | copy-start | bytes 786436
  190.8 0.7 copy-start.3
  200.1 206.2 %copy-start.12 = (bf16[1,2048,176]{1,2,0:T(8,128)(2,1)S(1)}, bf16[1,2048,176]{1,2,0:T(8,128)(2,1)}, u32[]{:S(2)}) copy-start(bf16[1,2048,176]{1,2,0:T(8,128)(2,1)} %param.22) | copy-start | bytes 2162692
  404.5 1.9 copy-start.1
  418.9 5.9 copy-start.4
  418.9 5.9 copy-start.13
  418.9 196.6 %all-to-all-start.2 = ((bf16[64,9,2048]{2,1,0:T(8,128)(2,1)}), bf16[64,9,2048]{2,1,0:T(8,128)(2,1)}, u32[]{:S(2)}, u32[]{:S(2)}) async-start(bf16[64,9,2048]{2,1,0:T(8,128)(2,1)} %copy.64), calls=%async_computation.2 | async-start | bytes 8388608 | tf_op jit(solution)/shard_map/all_to_all | solution.py:150
  424.7 282.0 %reduce-scatter.2.cloned.1.call-start = ((), (), s32[]{:S(2)}) async-start(), calls=%async_computation.5 | async-start | bytes 294912 | tf_op jit(solution)/shard_map/reduce_scatter | solution.py:155
Sparse Core Ops, SparseCore 0:
  96.7 91.8 all-reduce.2
  630.5 76.1 reduce-scatter.1
